TPU v7x, 512 devices: a whole 4x8x8 slice. The times are simulated.
512 devices in a mesh: blk: 64 (over x, y, z_hi), uly: 8 (over z_lo, core).
Axes of the slice: x: 4, y: 8, z: 8 (z_hi: 2, z_lo: 4; z = z_hi * 4 + z_lo), core: 2. Of those that a mesh axis runs over, the one named last changes fastest.
Arguments:
- residual: bfloat16 [6144, 2048], P(('blk', 'uly')), may hold values from -24 to 24
- query_projection: bfloat16 [6144, 4096], P(('blk', 'uly')), may hold values from -51 to 51
- key_projection: bfloat16 [6144, 1024], P(('blk', 'uly')), may hold values from -5.1 to 5.1
- value_projection: bfloat16 [6144, 1024], P(('blk', 'uly')), may hold values from -6 to 6
- gate_proj: bfloat16 [6144, 4096], P(('blk', 'uly')), may hold values from -6 to 6
- positions: int32 [6144], replicated, may hold values from 0 to 6143, each once
- prefix_len: int32 [1], replicated, may hold values from 768 to 3071
- out_weight: bfloat16 [4096, 2048], P('uly', 'blk'), may hold values from -0.375 to 0.375
- norm_gain: float32 [2048], replicated, may hold values from 0.1 to 1.9
- gate_weight: bfloat16 [2048, 6144], P('blk', 'uly'), may hold values from -0.125 to 0.125
- up_weight: bfloat16 [2048, 6144], P('blk', 'uly'), may hold values from -0.125 to 0.125
- down_weight: bfloat16 [6144, 2048], P('uly', 'blk'), may hold values from -0.078125 to 0.078125
Outputs:
- layer_out: bfloat16 [6144, 2048], P(('blk', 'uly'))
Inputs may be any that keep to these rules, and one draw needn't show every extreme that they name: `positions`: each of 0 to 6143 appears once.
All inputs are finite; a program needn't handle non-finite values.
Results may differ from a plain program's by a relative error of at most 0.014.
Values may be sent and summed in bfloat16 or wider, within the bound.
A program may use at most 64 MiB of HBM per device.

v0:
```python
import math
import jax
import jax.numpy as jnp
from jax import lax
from jax.sharding import PartitionSpec as P

HEAD_SIZE = 128


def per_device(
    residual,
    query_projection,
    key_projection,
    value_projection,
    gate_proj,
    positions,
    prefix_len,
    out_weight,
    norm_gain,
    gate_weight,
    up_weight,
    down_weight,
):
    q_loc, k_loc, v_loc, g_loc = (
        lax.all_to_all(query_projection, "uly", split_axis=1, concat_axis=0, tiled=True),
        lax.all_to_all(key_projection, "uly", split_axis=1, concat_axis=0, tiled=True),
        lax.all_to_all(value_projection, "uly", split_axis=1, concat_axis=0, tiled=True),
        lax.all_to_all(gate_proj, "uly", split_axis=1, concat_axis=0, tiled=True),
    )
    row_count = q_loc.shape[0]
    kv_heads = k_loc.shape[1] // HEAD_SIZE
    q_heads = q_loc.shape[1] // HEAD_SIZE
    heads_per_group = q_heads // kv_heads
    score_scale = 1.0 / math.sqrt(HEAD_SIZE)
    blk_index = lax.axis_index("blk")
    query_pos = lax.dynamic_slice_in_dim(positions, blk_index * row_count, row_count)
    prefix = prefix_len[0]
    query_heads = q_loc.reshape(row_count, kv_heads, heads_per_group, HEAD_SIZE)
    wo_full, wg_full, wu_full, wd_full = (
        lax.all_gather(out_weight, "blk", axis=1, tiled=True),
        lax.all_gather(gate_weight, "blk", axis=0, tiled=True),
        lax.all_gather(up_weight, "blk", axis=0, tiled=True),
        lax.all_gather(down_weight, "blk", axis=1, tiled=True),
    )
    run_max = jnp.full((row_count, kv_heads, heads_per_group), -jnp.inf, jnp.float32)
    run_sum = jnp.zeros((row_count, kv_heads, heads_per_group), jnp.float32)
    weighted = jnp.zeros((row_count, kv_heads, heads_per_group, HEAD_SIZE), jnp.float32)
    key_part = lax.all_gather(k_loc, "blk", axis=0, tiled=True)
    value_part = lax.all_gather(v_loc, "blk", axis=0, tiled=True)
    key_count = key_part.shape[0]
    scores = (
        jnp.einsum(
            "bkgd,skd->bkgs",
            query_heads,
            key_part.reshape(key_count, kv_heads, HEAD_SIZE),
            preferred_element_type=jnp.float32,
        )
        * score_scale
    )
    visible = (positions[None, :] <= query_pos[:, None]) | (positions[None, :] < prefix)
    scores = jnp.where(visible[:, None, None, :], scores, -jnp.inf)
    new_max = jnp.max(scores, axis=-1)
    safe_max = jnp.where(new_max == -jnp.inf, 0.0, new_max)
    factor = jnp.exp(run_max - safe_max)
    exp_scores = jnp.exp(scores - safe_max[..., None])
    run_sum = run_sum * factor + jnp.sum(exp_scores, axis=-1)
    probs = exp_scores.astype(jnp.bfloat16)
    weighted = weighted * factor[..., None] + jnp.einsum(
        "bkgs,skd->bkgd",
        probs,
        value_part.reshape(key_count, kv_heads, HEAD_SIZE),
        preferred_element_type=jnp.float32,
    )
    _, denom, weighted = (new_max, run_sum, weighted)
    attended = (weighted / denom[..., None]).reshape(row_count, q_heads * HEAD_SIZE)
    gated_out = (attended * jax.nn.sigmoid(g_loc.astype(jnp.float32))).astype(jnp.bfloat16)
    head_partial = jnp.dot(gated_out, wo_full, preferred_element_type=jnp.float32)
    projected = lax.psum_scatter(
        head_partial.astype(jnp.bfloat16), "uly", scatter_dimension=0, tiled=True
    ).astype(jnp.float32)
    hidden_f = (residual.astype(jnp.float32) + projected).astype(jnp.bfloat16).astype(jnp.float32)
    mean_sq = jnp.mean(hidden_f * hidden_f, axis=-1, keepdims=True)
    normed = (hidden_f * lax.rsqrt(mean_sq + 1e-06) * norm_gain).astype(jnp.bfloat16)
    group_rows = lax.all_gather(normed, "uly", axis=0, tiled=True)
    gate_sum = jnp.dot(group_rows, wg_full, preferred_element_type=jnp.float32)
    up_sum = jnp.dot(group_rows, wu_full, preferred_element_type=jnp.float32)
    activated = (jax.nn.silu(gate_sum) * up_sum).astype(jnp.bfloat16)
    ffn_partial = jnp.dot(activated, wd_full, preferred_element_type=jnp.float32)
    ffn_out = lax.psum_scatter(
        ffn_partial.astype(jnp.bfloat16), "uly", scatter_dimension=0, tiled=True
    ).astype(jnp.float32)
    return (hidden_f + ffn_out).astype(jnp.bfloat16)


def solution(mesh):
    return jax.shard_map(
        per_device,
        mesh=mesh,
        in_specs=(
            P(("blk", "uly"), None),
            P(("blk", "uly"), None),
            P(("blk", "uly"), None),
            P(("blk", "uly"), None),
            P(("blk", "uly"), None),
            P(),
            P(),
            P("uly", "blk"),
            P(),
            P("blk", "uly"),
            P("blk", "uly"),
            P("uly", "blk"),
        ),
        out_specs=P(("blk", "uly"), None),
        check_vma=False,
    )
```

profile of v0, /device:TPU:1, one launch (start us, length us, event | category | flops | bytes accessed | tf_op | source)
XLA Modules:
  0.0 897.3 jit_solution(13046254227862782462)
XLA Ops:
  6.5 0.8 copy.27
  7.3 14.2 %all_to_all.67 = bf16[12,8,128]{2,0,1:T(8,128)(2,1)S(1)} all-to-all(bf16[12,8,128]{2,0,1:T(8,128)(2,1)S(1)} %copy.21), channel_id=1, replica_groups=mesh['blk'=64,'uly'=8] {'uly'}, dimensions={1} | all-to-all | bytes 49152 | tf_op jit(solution)/shard_map/all_to_all | solution.py:26
  21.5 0.6 all_to_all.53
  22.1 0.0 all-gather.8.cloned.1.call-update
  22.1 0.0 all-gather.10.cloned.1.call-start
  22.2 0.8 copy.29
  23.0 8.1 all_to_all.68
  31.1 0.6 all_to_all.60
  31.7 0.0 all-gather.10.cloned.1.call-update
  31.7 0.0 all-gather.12.cloned.1.call-start
  31.8 0.7 all-gather.12.cloned.1.call-update
  32.5 0.0 all-gather.14.cloned.1.call-start
  32.5 0.5 all-gather.14.cloned.1.call-update
  33.0 0.0 all-gather.16.cloned.1.call-start
  33.1 0.5 all-gather.16.cloned.1.call-update
  33.6 0.9 copy.28
  34.6 0.7 copy.22
  35.3 4.0 all-to-all-start.1
  39.3 0.0 all-gather.18.cloned.1.call-start
  39.3 0.6 all-gather.18.cloned.1.call-update
  40.5 0.9 copy.31
  41.5 0.7 copy.26
  42.2 0.8 dynamic_slice.3
  43.0 0.7 broadcast_compare_fusion
  43.7 1.5 all-to-all-done.1
  45.2 4.3 all-to-all-start.3
  49.6 1.2 compare_or_fusion
  50.8 4.6 all-to-all-done.3
  55.4 0.1 divide_bitcast_fusion
  55.5 97.2 %all-gather.8.cloned.1.call-done = bf16[6144,128]{1,0:T(8,128)(2,1)} async-done(((bf16[96,128]{1,0:T(8,128)(2,1)}), bf16[6144,128]{1,0:T(8,128)(2,1)}) %all-gather.8.cloned.1.call-update) | async-done | bytes 1572880 | tf_op jit(solution)/shard_map/all_gather | solution.py:48
  152.7 3.3 fusion.47
  156.0 1.4 fusion.2
  157.4 2.2 copy-done
  159.7 124.8 %all-gather.10.cloned.1.call-done = bf16[6144,128]{1,0:T(8,128)(2,1)} async-done(((bf16[96,128]{1,0:T(8,128)(2,1)}), bf16[6144,128]{1,0:T(8,128)(2,1)}) %all-gather.10.cloned.1.call-update) | async-done | bytes 1572880 | tf_op jit(solution)/shard_map/all_gather | solution.py:49
  284.4 5.6 fusion.26
  290.0 0.0 copy-start.1
  290.0 0.0 copy-start.2
  290.0 0.1 copy.25
  290.1 131.4 %all-gather.12.cloned.1.call-done = bf16[512,2048]{0,1:T(8,128)(2,1)} async-done(((bf16[512,32]{0,1:T(8,128)(2,1)}), bf16[512,2048]{0,1:T(8,128)(2,1)}) %all-gather.12.cloned.1.call-update) | async-done | bytes 2097168 | tf_op jit(solution)/shard_map/all_gather | solution.py:40
  421.6 2.3 convolution_convert_fusion
  423.9 21.0 %fusion = bf16[16,2048]{1,0:T(8,128)(2,1)S(1)} fusion(bf16[96,2048]{1,0:T(8,128)(2,1)S(1)} %convolution_convert_fusion), kind=kCustom, calls=%all-reduce-scatter | all-reduce-scatter fusion | flops 262145 | bytes 460800
  445.0 1.9 collective-permute-start
  446.9 2.2 collective-permute-start.1
  449.1 1.3 dynamic-slice.6
  451.1 0.0 collective-permute-done.1
  451.1 0.0 collective-permute-done
  451.1 0.4 concatenate
  451.5 0.2 fusion.38
  451.7 0.0 copy-done.2
  451.7 0.1 fusion.44
  451.8 15.2 %all-gather = bf16[8,12,2048]{2,1,0:T(8,128)(2,1)S(1)} all-gather(bf16[1,12,2048]{2,1,0:T(8,128)(2,1)S(1)} %fusion.44), channel_id=1, replica_groups=mesh['blk'=64,'uly'=8] {'uly'}, dimensions={0}, use_global_device_ids=true | all-gather | bytes 442368 | tf_op jit(solution)/shard_map/all_gather | solution.py:84
  467.0 0.1 reshape.132
  467.1 100.4 %all-gather.14.cloned.1.call-done = bf16[2048,768]{1,0:T(8,128)(2,1)} async-done(((bf16[32,768]{1,0:T(8,128)(2,1)}), bf16[2048,768]{1,0:T(8,128)(2,1)}) %all-gather.14.cloned.1.call-update) | async-done | bytes 3145744 | tf_op jit(solution)/shard_map/all_gather | solution.py:41
  567.5 2.5 fusion.48
  570.0 143.2 %all-gather.16.cloned.1.call-done = bf16[2048,768]{1,0:T(8,128)(2,1)} async-done(((bf16[32,768]{1,0:T(8,128)(2,1)}), bf16[2048,768]{1,0:T(8,128)(2,1)}) %all-gather.16.cloned.1.call-update) | async-done | bytes 3145744 | tf_op jit(solution)/shard_map/all_gather | solution.py:42
  713.3 145.8 %all-gather.18.cloned.1.call-done = bf16[768,2048]{0,1:T(8,128)(2,1)} async-done(((bf16[768,32]{0,1:T(8,128)(2,1)}), bf16[768,2048]{0,1:T(8,128)(2,1)}) %all-gather.18.cloned.1.call-update) | async-done | bytes 3145744 | tf_op jit(solution)/shard_map/all_gather | solution.py:43
  859.0 4.6 convolution_convert_fusion.1
  863.6 20.3 %fusion.1 = bf16[16,2048]{1,0:T(8,128)(2,1)S(1)} fusion(bf16[96,2048]{1,0:T(8,128)(2,1)S(1)} %convolution_convert_fusion.1), kind=kCustom, calls=%all-reduce-scatter.1 | all-reduce-scatter fusion | flops 262145 | bytes 460800
  883.9 1.9 collective-permute-start.2
  885.8 2.3 collective-permute-start.3
  888.1 1.3 collective-permute-done.3
  889.4 0.0 collective-permute-done.2
  889.4 0.4 concatenate.1
  889.8 0.7 fusion.41
  (16 shorter events, 0.2 us)
Async XLA Ops:
  6.5 146.1 %all-gather.8.cloned.1.call-start = ((), (), s32[]{:S(2)}) async-start(), calls=%async_computation.4 | async-start | bytes 1597440 | tf_op jit(solution)/shard_map/all_gather | solution.py:48
  22.1 262.3 %all-gather.10.cloned.1.call-start = ((), (), s32[]{:S(2)}) async-start(), calls=%async_computation.5 | async-start | bytes 1597440 | tf_op jit(solution)/shard_map/all_gather | solution.py:49
  31.7 389.9 %all-gather.12.cloned.1.call-start = ((), (), s32[]{:S(2)}) async-start(), calls=%async_computation.6 | async-start | bytes 2129920 | tf_op jit(solution)/shard_map/all_gather | solution.py:40
  32.5 535.0 %all-gather.14.cloned.1.call-start = ((), (), s32[]{:S(2)}) async-start(), calls=%async_computation.7 | async-start | bytes 3194880 | tf_op jit(solution)/shard_map/all_gather | solution.py:41
  33.0 680.2 %all-gather.16.cloned.1.call-start = ((), (), s32[]{:S(2)}) async-start(), calls=%async_computation.8 | async-start | bytes 3194880 | tf_op jit(solution)/shard_map/all_gather | solution.py:42
  35.3 10.0 %all-to-all-start.1 = ((bf16[12,8,512]{2,0,1:T(8,128)(2,1)}), bf16[12,8,512]{2,0,1:T(8,128)(2,1)S(1)}, u32[]{:S(2)}, u32[]{:S(2)}) async-start(bf16[12,8,512]{2,0,1:T(8,128)(2,1)} %copy.22), calls=%async_computation.1 | async-start | bytes 262144 | tf_op jit(solution)/shard_map/all_to_all | solution.py:25
  39.3 819.7 %all-gather.18.cloned.1.call-start = ((), (), s32[]{:S(2)}) async-start(), calls=%async_computation.9 | async-start | bytes 3194880 | tf_op jit(solution)/shard_map/all_gather | solution.py:43
  45.2 10.2 %all-to-all-start.3 = ((bf16[12,8,512]{2,0,1:T(8,128)(2,1)}), bf16[12,8,512]{2,0,1:T(8,128)(2,1)S(1)}, u32[]{:S(2)}, u32[]{:S(2)}) async-start(bf16[12,8,512]{2,0,1:T(8,128)(2,1)} %copy.26), calls=%async_computation.3 | async-start | bytes 262144 | tf_op jit(solution)/shard_map/all_to_all | solution.py:28
  156.0 3.7 copy-start
  290.0 161.5 %copy-start.1 = (bf16[12,2048]{1,0:T(8,128)(2,1)S(1)}, bf16[12,2048]{1,0:T(8,128)(2,1)}, u32[]{:S(2)}) copy-start(bf16[12,2048]{1,0:T(8,128)(2,1)} %param.12) | copy-start | bytes 147460
  290.0 161.7 %copy-start.2 = (f32[2048]{0:T(1024)S(1)}, f32[2048]{0:T(1024)}, u32[]{:S(2)}) copy-start(f32[2048]{0:T(1024)} %param.20) | copy-start | bytes 24580
  445.0 6.1 collective-permute-start
  446.9 4.1 collective-permute-start.1
  883.9 5.5 collective-permute-start.2
  885.8 3.6 collective-permute-start.3
Sparse Core Ops, SparseCore 0:
  22.3 130.3 all-gather.7
  157.1 127.2 all-gather.9
  288.9 132.6 all-gather.11
  425.9 141.5 all-gather.13
  571.8 141.4 all-gather.15
  717.6 141.4 all-gather.17
where the time goes:
time: 898 us; the launch traced here: 897 us
  waiting for transfers between devices  753 us (84%)
  blocking collectives  78.8 us (9%)
  matrix products  18.3 us (2%)
  starting transfers between devices  16.9 us (2%)
  between operations  15 us (2%)
  local copies, waits for them, and re-layouts  11.4 us (1%)
    all_gather x1, waiting for transfers between devices, per_device(): lax.all_gather(down_weight, 'blk', axis=1, tiled=True)  146 us
    all_gather x1, waiting for transfers between devices, per_device(): lax.all_gather(up_weight, 'blk', axis=0, tiled=True)  143 us
    all_gather x1, waiting for transfers between devices, per_device(): lax.all_gather(out_weight, 'blk', axis=1, tiled=True)  131 us
    all_gather x1, waiting for transfers between devices, per_device(): value_part = lax.all_gather(v_loc, 'blk', axis=0, tiled=True)  125 us
    all_gather x1, waiting for transfers between devices, per_device(): lax.all_gather(gate_weight, 'blk', axis=0, tiled=True)  100 us
    all_gather x1, waiting for transfers between devices, per_device(): key_part = lax.all_gather(k_loc, 'blk', axis=0, tiled=True)  97.2 us
    unnamed x2, blocking collectives  41.3 us
  transfers between devices with their start and end apart: 12, of which 9 were waited for; matrix products, arithmetic and copies ran while one was open for 5% of the time, Pallas kernels for 0%

commit v1 on v0

--- a/solution.py
+++ b/solution.py
@@ -45,7 +45,9 @@
     run_max = jnp.full((row_count, kv_heads, heads_per_group), -jnp.inf, jnp.float32)
     run_sum = jnp.zeros((row_count, kv_heads, heads_per_group), jnp.float32)
     weighted = jnp.zeros((row_count, kv_heads, heads_per_group, HEAD_SIZE), jnp.float32)
-    key_part = lax.all_gather(k_loc, "blk", axis=0, tiled=True)
+    key_part = jnp.concatenate(
+        lax.all_to_all(jnp.stack([k_loc] * lax.axis_size("blk")), "blk", 0, 0), axis=0
+    )
     value_part = lax.all_gather(v_loc, "blk", axis=0, tiled=True)
     key_count = key_part.shape[0]
     scores = (

time: 898 us -> 790 us (0.88)
  waiting for transfers between devices: 753 us -> 636 us
  starting transfers between devices: 16.9 us -> 36.2 us
    all_gather x1 -> x0, waiting for transfers between devices: 97.2 us -> none  [per_device(): key_part = lax.all_gather(k_loc, 'blk', axis=0, tiled=True)]
    all_gather x1, waiting for transfers between devices: 125 us -> 56.8 us  [per_device(): value_part = lax.all_gather(v_loc, 'blk', axis=0, tiled=True)]
    all_to_all x0 -> x2, waiting for transfers between devices: none -> 44 us  [the longest x1 40.7 us: per_device(): lax.all_to_all(jnp.stack([k_loc] * lax.axis_size('blk')), 'blk', 0, 0)]
    all_to_all x0 -> x2, starting transfers between devices: none -> 19.3 us  [the longest x1 15.3 us: per_device(): lax.all_to_all(jnp.stack([k_loc] * lax.axis_size('blk')), 'blk', 0, 0)]
    all_to_all x1 -> x0, blocking collectives: 14.2 us -> none  [per_device(): lax.all_to_all(key_projection, 'uly', split_axis=1, concat_axis=0, tiled=...]
  transfers between devices with their start and end apart: 12 -> 13, of which waited for: 9 -> 10; matrix products, arithmetic and copies ran while one was open for 5% -> 6% of each run, Pallas kernels for 0% -> 0%
where the time goes in v1:
time: 790 us; the launch traced here: 789 us
  waiting for transfers between devices  636 us (81%)
  blocking collectives  70.8 us (9%)
  starting transfers between devices  36.2 us (5%)
  matrix products  16.8 us (2%)
  between operations  14.7 us (2%)
  local copies, waits for them, and re-layouts  12.1 us (2%)
    all_gather x1, waiting for transfers between devices, per_device(): lax.all_gather(down_weight, 'blk', axis=1, tiled=True)  146 us
    all_gather x1, waiting for transfers between devices, per_device(): lax.all_gather(up_weight, 'blk', axis=0, tiled=True)  143 us
    all_gather x1, waiting for transfers between devices, per_device(): lax.all_gather(out_weight, 'blk', axis=1, tiled=True)  131 us
    all_gather x1, waiting for transfers between devices, per_device(): lax.all_gather(gate_weight, 'blk', axis=0, tiled=True)  100 us
    all_gather x1, waiting for transfers between devices, per_device(): value_part = lax.all_gather(v_loc, 'blk', axis=0, tiled=True)  56.8 us
    unnamed x2, blocking collectives  41.3 us
    all_to_all x1, waiting for transfers between devices, per_device(): lax.all_to_all(jnp.stack([k_loc] * lax.axis_size('blk')), 'blk', 0, 0)  40.7 us
  transfers between devices with their start and end apart: 13, of which 10 were waited for; matrix products, arithmetic and copies ran while one was open for 6% of the time, Pallas kernels for 0%

profile of v1, /device:TPU:1, one launch (start us, length us, event | category | flops | bytes accessed | tf_op | source)
XLA Modules:
  0.0 789.0 jit_solution(9402865728141464766)
XLA Ops:
  6.5 0.8 copy.28
  7.3 14.2 %all_to_all.69 = bf16[12,8,128]{2,0,1:T(8,128)(2,1)S(1)} all-to-all(bf16[12,8,128]{2,0,1:T(8,128)(2,1)S(1)} %copy.23), channel_id=1, replica_groups=mesh['blk'=64,'uly'=8] {'uly'}, dimensions={1} | all-to-all | bytes 49152 | tf_op jit(solution)/shard_map/all_to_all | solution.py:27
  21.5 0.6 all_to_all.61
  22.1 0.0 all-gather.7.cloned.1.call-update
  22.1 0.0 all-gather.9.cloned.1.call-start
  22.2 0.7 all-gather.9.cloned.1.call-update
  22.9 0.0 all-gather.11.cloned.1.call-start
  22.9 0.7 all-gather.11.cloned.1.call-update
  23.6 0.0 all-gather.13.cloned.1.call-start
  23.7 0.5 all-gather.13.cloned.1.call-update
  24.2 0.8 copy.26
  25.0 0.6 copy.20
  25.6 4.0 all-to-all-start
  29.6 0.9 copy.27
  30.6 0.0 copy-start.1
  30.6 0.7 copy.21
  31.3 3.3 all-to-all-done
  34.6 4.0 all-to-all-start.2
  38.7 0.9 copy.30
  39.6 0.7 copy.25
  40.3 4.2 all-to-all-done.2
  44.5 4.3 all-to-all-start.4
  48.8 5.8 all-to-all-done.4
  54.6 1.4 stack.5
  56.0 15.3 %all-to-all-start.1 = ((bf16[64,96,128]{2,1,0:T(8,128)(2,1)}), bf16[64,96,128]{2,1,0:T(8,128)(2,1)S(1)}, u32[]{:S(2)}, u32[]{:S(2)}) async-start(bf16[64,96,128]{2,1,0:T(8,128)(2,1)} %stack.5), calls=%async_computation.1 | async-start | bytes 3145728 | tf_op jit(solution)/shard_map/all_to_all | solution.py:49
  71.3 0.0 all-gather.15.cloned.1.call-start
  71.4 0.5 all-gather.15.cloned.1.call-update
  72.6 0.1 dynamic_slice.3
  72.7 0.5 compare_or_fusion
  73.2 0.1 divide_bitcast_fusion
  73.3 40.7 %all-to-all-done.1 = bf16[64,96,128]{2,1,0:T(8,128)(2,1)S(1)} async-done(((bf16[64,96,128]{2,1,0:T(8,128)(2,1)}), bf16[64,96,128]{2,1,0:T(8,128)(2,1)S(1)}, u32[]{:S(2)}, u32[]{:S(2)}) %all-to-all-start.1) | async-done | bytes 1572896 | tf_op jit(solution)/shard_map/all_to_all | solution.py:49
  114.0 1.8 fusion.46
  115.8 1.4 fusion.2
  117.3 2.2 copy-done
  119.5 56.8 %all-gather.7.cloned.1.call-done = bf16[6144,128]{1,0:T(8,128)(2,1)} async-done(((bf16[96,128]{1,0:T(8,128)(2,1)}), bf16[6144,128]{1,0:T(8,128)(2,1)}) %all-gather.7.cloned.1.call-update) | async-done | bytes 1572880 | tf_op jit(solution)/shard_map/all_gather | solution.py:51
  176.3 5.6 fusion.25
  181.9 0.0 copy-start.2
  181.9 0.0 copy-start.3
  181.9 0.1 copy.24
  182.1 131.4 %all-gather.9.cloned.1.call-done = bf16[512,2048]{0,1:T(8,128)(2,1)} async-done(((bf16[512,32]{0,1:T(8,128)(2,1)}), bf16[512,2048]{0,1:T(8,128)(2,1)}) %all-gather.9.cloned.1.call-update) | async-done | bytes 2097168 | tf_op jit(solution)/shard_map/all_gather | solution.py:40
  313.5 2.4 convolution_convert_fusion
  315.9 21.0 %fusion = bf16[16,2048]{1,0:T(8,128)(2,1)S(1)} fusion(bf16[96,2048]{1,0:T(8,128)(2,1)S(1)} %convolution_convert_fusion), kind=kCustom, calls=%all-reduce-scatter | all-reduce-scatter fusion | flops 262145 | bytes 460800
  336.9 1.9 collective-permute-start
  338.8 2.2 collective-permute-start.1
  341.0 1.3 dynamic-slice.6
  343.0 0.0 collective-permute-done.1
  343.0 0.0 collective-permute-done
  343.0 0.4 concatenate
  343.4 0.2 fusion.37
  343.6 0.1 fusion.43
  343.7 15.3 %all-gather = bf16[8,12,2048]{2,1,0:T(8,128)(2,1)S(1)} all-gather(bf16[1,12,2048]{2,1,0:T(8,128)(2,1)S(1)} %fusion.43), channel_id=1, replica_groups=mesh['blk'=64,'uly'=8] {'uly'}, dimensions={0}, use_global_device_ids=true | all-gather | bytes 442368 | tf_op jit(solution)/shard_map/all_gather | solution.py:86
  359.0 0.1 reshape.137
  359.0 100.5 %all-gather.11.cloned.1.call-done = bf16[2048,768]{1,0:T(8,128)(2,1)} async-done(((bf16[32,768]{1,0:T(8,128)(2,1)}), bf16[2048,768]{1,0:T(8,128)(2,1)}) %all-gather.11.cloned.1.call-update) | async-done | bytes 3145744 | tf_op jit(solution)/shard_map/all_gather | solution.py:41
  459.5 2.5 fusion.47
  462.1 143.3 %all-gather.13.cloned.1.call-done = bf16[2048,768]{1,0:T(8,128)(2,1)} async-done(((bf16[32,768]{1,0:T(8,128)(2,1)}), bf16[2048,768]{1,0:T(8,128)(2,1)}) %all-gather.13.cloned.1.call-update) | async-done | bytes 3145744 | tf_op jit(solution)/shard_map/all_gather | solution.py:42
  605.3 145.8 %all-gather.15.cloned.1.call-done = bf16[768,2048]{0,1:T(8,128)(2,1)} async-done(((bf16[768,32]{0,1:T(8,128)(2,1)}), bf16[768,2048]{0,1:T(8,128)(2,1)}) %all-gather.15.cloned.1.call-update) | async-done | bytes 3145744 | tf_op jit(solution)/shard_map/all_gather | solution.py:43
  751.1 4.5 convolution_convert_fusion.1
  755.6 20.3 %fusion.1 = bf16[16,2048]{1,0:T(8,128)(2,1)S(1)} fusion(bf16[96,2048]{1,0:T(8,128)(2,1)S(1)} %convolution_convert_fusion.1), kind=kCustom, calls=%all-reduce-scatter.1 | all-reduce-scatter fusion | flops 262145 | bytes 460800
  775.9 1.9 collective-permute-start.2
  777.9 2.3 collective-permute-start.3
  780.1 1.3 collective-permute-done.3
  781.4 0.0 collective-permute-done.2
  781.4 0.4 concatenate.1
  781.8 0.7 fusion.40
  (19 shorter events, 0.2 us)
Async XLA Ops:
  6.5 169.8 %all-gather.7.cloned.1.call-start = ((), (), s32[]{:S(2)}) async-start(), calls=%async_computation.5 | async-start | bytes 1597440 | tf_op jit(solution)/shard_map/all_gather | solution.py:51
  22.1 291.4 %all-gather.9.cloned.1.call-start = ((), (), s32[]{:S(2)}) async-start(), calls=%async_computation.6 | async-start | bytes 2129920 | tf_op jit(solution)/shard_map/all_gather | solution.py:40
  22.9 436.7 %all-gather.11.cloned.1.call-start = ((), (), s32[]{:S(2)}) async-start(), calls=%async_computation.7 | async-start | bytes 3194880 | tf_op jit(solution)/shard_map/all_gather | solution.py:41
  23.6 581.7 %all-gather.13.cloned.1.call-start = ((), (), s32[]{:S(2)}) async-start(), calls=%async_computation.8 | async-start | bytes 3194880 | tf_op jit(solution)/shard_map/all_gather | solution.py:42
  25.6 9.0 %all-to-all-start = ((bf16[12,8,128]{2,0,1:T(8,128)(2,1)}), bf16[12,8,128]{2,0,1:T(8,128)(2,1)S(1)}, u32[]{:S(2)}, u32[]{:S(2)}) async-start(bf16[12,8,128]{2,0,1:T(8,128)(2,1)} %copy.20), calls=%async_computation | async-start | bytes 65536 | tf_op jit(solution)/shard_map/all_to_all | solution.py:26
  30.6 42.0 %copy-start.1 = (s32[6144]{0:T(1024)S(1)}, s32[6144]{0:T(1024)}, u32[]{:S(2)}) copy-start(s32[6144]{0:T(1024)} %param.17) | copy-start | bytes 73732
  34.6 9.9 %all-to-all-start.2 = ((bf16[12,8,512]{2,0,1:T(8,128)(2,1)}), bf16[12,8,512]{2,0,1:T(8,128)(2,1)S(1)}, u32[]{:S(2)}, u32[]{:S(2)}) async-start(bf16[12,8,512]{2,0,1:T(8,128)(2,1)} %copy.21), calls=%async_computation.2 | async-start | bytes 262144 | tf_op jit(solution)/shard_map/all_to_all | solution.py:25
  44.5 10.1 %all-to-all-start.4 = ((bf16[12,8,512]{2,0,1:T(8,128)(2,1)}), bf16[12,8,512]{2,0,1:T(8,128)(2,1)S(1)}, u32[]{:S(2)}, u32[]{:S(2)}) async-start(bf16[12,8,512]{2,0,1:T(8,128)(2,1)} %copy.25), calls=%async_computation.4 | async-start | bytes 262144 | tf_op jit(solution)/shard_map/all_to_all | solution.py:28
  56.0 58.0 %all-to-all-start.1 = ((bf16[64,96,128]{2,1,0:T(8,128)(2,1)}), bf16[64,96,128]{2,1,0:T(8,128)(2,1)S(1)}, u32[]{:S(2)}, u32[]{:S(2)}) async-start(bf16[64,96,128]{2,1,0:T(8,128)(2,1)} %stack.5), calls=%async_computation.1 | async-start | bytes 3145728 | tf_op jit(solution)/shard_map/all_to_all | solution.py:49
  71.3 679.7 %all-gather.15.cloned.1.call-start = ((), (), s32[]{:S(2)}) async-start(), calls=%async_computation.9 | async-start | bytes 3194880 | tf_op jit(solution)/shard_map/all_gather | solution.py:43
  115.8 3.7 copy-start
  181.9 161.5 %copy-start.2 = (bf16[12,2048]{1,0:T(8,128)(2,1)S(1)}, bf16[12,2048]{1,0:T(8,128)(2,1)}, u32[]{:S(2)}) copy-start(bf16[12,2048]{1,0:T(8,128)(2,1)} %param.12) | copy-start | bytes 147460
  181.9 161.6 %copy-start.3 = (f32[2048]{0:T(1024)S(1)}, f32[2048]{0:T(1024)}, u32[]{:S(2)}) copy-start(f32[2048]{0:T(1024)} %param.20) | copy-start | bytes 24580
  336.9 6.1 collective-permute-start
  338.8 4.1 collective-permute-start.1
  775.9 5.5 collective-permute-start.2
  777.9 3.6 collective-permute-start.3
Sparse Core Ops, SparseCore 0:
  22.3 154.0 all-gather.6
  180.8 132.6 all-gather.8
  317.9 141.5 all-gather.10
  463.8 141.4 all-gather.12
  609.6 141.4 all-gather.14
